TPU v7x, 128 devices: a whole 4x4x4 slice. The times are simulated.
128 devices in a mesh: seq: 64 (over z, y, x), exp: 2 (over core).
Axes of the slice: x: 4, y: 4, z: 4, core: 2. Of those that a mesh axis runs over, the one named last changes fastest.
Arguments:
- queries: bfloat16 [16384, 1024], P('seq', 'exp'), may hold values from -170 to 170
- keys: bfloat16 [16384, 1024], P('seq', 'exp'), may hold values from -5 to 5
- values: bfloat16 [16384, 1024], P('seq', 'exp'), may hold values from -6 to 6
- resid: bfloat16 [16384, 2048], P(('seq', 'exp')), may hold values from -6 to 6
- pair_ids: int32 [16384], replicated, may hold values from 0 to 63, never falling along the last dimension, each value on 1 to 512 neighbouring positions
- out_weight: bfloat16 [1024, 2048], P('exp'), may hold values from -0.1875 to 0.1875
- norm_gain: float32 [2048], replicated, may hold values from 0.5 to 1.5
- experts: int32 [16384, 6], P(('seq', 'exp')), may hold values from 0 to 63, all different within a row; in each aligned block of 128 rows (0 to 127, 128 to 255, ...) at most 24 rows name the same one
- gates: float32 [16384, 6], P(('seq', 'exp')), may hold values from 0.05 to 0.5
- w_gate: bfloat16 [64, 2048, 704], P('seq', None, 'exp'), may hold values from -0.125 to 0.125
- w_up: bfloat16 [64, 2048, 704], P('seq', None, 'exp'), may hold values from -0.125 to 0.125
- w_down: bfloat16 [64, 704, 2048], P('seq', 'exp'), may hold values from -0.21875 to 0.21875
Outputs:
- mixed: bfloat16 [16384, 2048], P(('seq', 'exp'))
Inputs may be any that keep to these rules, and one draw needn't show every extreme that they name: In the aligned blocks of 128 rows no expert is named more than 24 times, a bound that some block reaches; each row names 6 different experts. `pair_ids`: pair numbers never fall along the sequence; each pair has 1 to 512 tokens, one exactly that many.
All inputs are finite; a program needn't handle non-finite values.
Results may differ from a plain program's by a relative error of at most 0.012.
Values may be sent and summed in bfloat16 or wider, within the bound.
A program may use at most 128 MiB of HBM per device.

v0:
```python
import math
import jax
import jax.numpy as jnp
from jax import lax
from jax.sharding import PartitionSpec as P

HD = 128
TOP = 6


def with_halo(cells, sides, width):
    for axis, dim in sides:
        count = lax.axis_size(axis)
        ends = count - 1
        head = lax.slice_in_dim(cells, 0, width, axis=dim)
        tail = lax.slice_in_dim(cells, cells.shape[dim] - width, cells.shape[dim], axis=dim)
        cells = jnp.concatenate(
            [
                lax.ppermute(tail, axis, [(i, (i + 1) % count) for i in range(ends)]),
                cells,
                lax.ppermute(head, axis, [((i + 1) % count, i) for i in range(ends)]),
            ],
            axis=dim,
        )
    return cells


def send_back(result):
    return lax.all_to_all(result, "seq", split_axis=0, concat_axis=0, tiled=True)


def shards(
    queries,
    keys,
    values,
    resid,
    pair_ids,
    out_weight,
    norm_gain,
    experts,
    gates,
    w_gate,
    w_up,
    w_down,
):
    tok_rows = queries.shape[0]
    local_width = queries.shape[1]
    local_heads = local_width // HD
    shard = lax.axis_index("seq")
    stacked = jnp.stack([keys, values])
    widened = with_halo(stacked, (("seq", 1),), tok_rows)
    id_pad = jnp.pad(pair_ids, (tok_rows, tok_rows), constant_values=-1)
    key_ids = lax.dynamic_slice_in_dim(id_pad, shard * tok_rows, 3 * tok_rows, 0)
    query_ids = lax.dynamic_slice_in_dim(id_pad, shard * tok_rows + tok_rows, tok_rows, 0)
    query_pos = jnp.arange(tok_rows, dtype=jnp.int32) + tok_rows
    key_pos = jnp.arange(3 * tok_rows, dtype=jnp.int32)
    allowed = (query_ids[:, None] == key_ids[None, :]) & (
        jnp.abs(query_pos[:, None] - key_pos[None, :]) < tok_rows
    )
    query_heads = queries.reshape(tok_rows, local_heads, HD)
    key_heads = widened[0].reshape(3 * tok_rows, local_heads, HD)
    value_heads = widened[1].reshape(3 * tok_rows, local_heads, HD)
    score = jnp.einsum(
        "qhd,khd->hqk", query_heads, key_heads, preferred_element_type=jnp.float32
    ) / math.sqrt(HD)
    score = jnp.where(allowed[None], score, -jnp.inf)
    top = jnp.max(score, axis=-1, keepdims=True)
    weights = jnp.exp(score - top)
    probs = (weights / jnp.sum(weights, axis=-1, keepdims=True)).astype(jnp.bfloat16)
    attended = jnp.einsum("hqk,khd->qhd", probs, value_heads, preferred_element_type=jnp.float32)
    attended = attended.reshape(tok_rows, local_width).astype(jnp.bfloat16)
    moe_rows = resid.shape[0]
    projected = lax.psum(
        jnp.dot(attended, out_weight, preferred_element_type=jnp.float32).astype(jnp.bfloat16),
        "exp",
    ).astype(jnp.float32)
    projected = lax.dynamic_slice_in_dim(projected, lax.axis_index("exp") * moe_rows, moe_rows, 0)
    stream = resid.astype(jnp.float32) + projected
    meansq = jnp.mean(stream * stream, axis=-1, keepdims=True)
    normed = (stream * lax.rsqrt(meansq + 1e-05) * norm_gain).astype(jnp.bfloat16)
    n_experts = lax.axis_size("seq") * w_gate.shape[0]
    capacity = 2 * moe_rows * TOP // n_experts
    flat_experts = experts.reshape(-1)
    onehot = (flat_experts[:, None] == jnp.arange(n_experts, dtype=jnp.int32)[None, :]).astype(
        jnp.int32
    )
    ranks = jnp.cumsum(onehot, axis=0) - onehot
    slot_index = jnp.sum(ranks * onehot, axis=1)
    destination = flat_experts * capacity + slot_index
    token_of = jnp.arange(moe_rows * TOP, dtype=jnp.int32) // TOP
    outgoing = (
        jnp.zeros((n_experts * capacity, normed.shape[1]), jnp.bfloat16)
        .at[destination]
        .set(normed[token_of])
    )
    outgoing = outgoing.reshape(n_experts, capacity, normed.shape[1])
    arrived = lax.all_to_all(outgoing, "seq", split_axis=0, concat_axis=0, tiled=True)
    sources = arrived.shape[0]
    slots = arrived.shape[1]
    inputs = arrived.reshape(sources * slots, arrived.shape[2])
    group = lax.all_gather(inputs, "exp", axis=0, tiled=True)
    gate_part = jnp.dot(group, w_gate[0], preferred_element_type=jnp.float32)
    up_part = jnp.dot(group, w_up[0], preferred_element_type=jnp.float32)
    act = (jax.nn.silu(gate_part) * up_part).astype(jnp.bfloat16)
    result = lax.psum_scatter(
        jnp.dot(act, w_down[0], preferred_element_type=jnp.float32).astype(jnp.bfloat16),
        "exp",
        scatter_dimension=0,
        tiled=True,
    )
    result = result.reshape(sources, slots, result.shape[1])
    back = send_back(result)
    gathered = back.reshape(n_experts * capacity, back.shape[2])[destination]
    gathered = gathered.reshape(moe_rows, TOP, gathered.shape[1]).astype(jnp.float32)
    mixture = jnp.einsum("mk,mkd->md", gates, gathered)
    return (stream + mixture).astype(jnp.bfloat16)


def solution(mesh):
    in_specs = (
        P("seq", "exp"),
        P("seq", "exp"),
        P("seq", "exp"),
        P(("seq", "exp"), None),
        P(),
        P("exp", None),
        P(),
        P(("seq", "exp"), None),
        P(("seq", "exp"), None),
        P("seq", None, "exp"),
        P("seq", None, "exp"),
        P("seq", "exp", None),
    )
    out_specs = P(("seq", "exp"), None)
    return jax.shard_map(shards, mesh=mesh, in_specs=in_specs, out_specs=out_specs, check_vma=False)
```

profile of v0, /device:TPU:10, one launch (start us, length us, event | category | flops | bytes accessed | tf_op | source)
XLA Modules:
  0.0 383.7 jit_solution(15358219397726013312)
XLA Ops:
  6.5 1.2 copy.16
  8.9 3.4 collective-permute-start
  12.3 2.4 collective-permute-start.1
  16.6 7.9 %collective-permute-done = bf16[2,256,512]{1,2,0:T(8,128)(2,1)} collective-permute-done((bf16[2,256,512]{1,2,0:T(8,128)(2,1)S(1)}, bf16[2,256,512]{1,2,0:T(8,128)(2,1)}, u32[]{:S(2)}, u32[]{:S(2)}) %collective-permute-start) | collective-permute-done | bytes 524320 | tf_op jit(solution)/shard_map/ppermute | solution.py:19
  24.6 3.1 collective-permute-done.1
  27.7 1.3 pad_maximum_fusion
  29.8 1.6 fusion.32
  31.8 1.7 convolution_convert_fusion.1
  34.1 1.8 reduce-window.6
  36.6 28.0 %all-reduce.3.cloned.1.call-done = bf16[256,2048]{1,0:T(8,128)(2,1)} async-done(((bf16[256,2048]{1,0:T(8,128)(2,1)}), bf16[256,2048]{1,0:T(8,128)(2,1)}) %all-reduce.3.cloned.1.call-update) | async-done | bytes 1048592 | tf_op jit(solution)/shard_map/psum | solution.py:73
  64.6 1.3 multiply_reduce_fusion
  65.9 1.3 multiply_convert_fusion
  67.2 24.2 %scatter_custom_fusion = bf16[1536,2048]{1,0:T(8,128)(2,1)} fusion(s32[768]{0:T(1024)S(1)} %fusion.26, bf16[128,2048]{1,0:T(8,128)(2,1)S(1)} %multiply_convert_fusion, s32[1024]{0:T(1024)S(1)} %pad_clamp_fusion.1, bf16[]{:T(256)} %constant.50.clone.1), kind=kCustom, calls=%fused_computation.8 | custom fusion | bytes 6291458 | tf_op jit(solution)/shard_map/scatter | solution.py:94
  91.4 84.0 %all_to_all.10 = bf16[64,24,2048]{2,1,0:T(8,128)(2,1)} all-to-all(bf16[64,24,2048]{2,1,0:T(8,128)(2,1)} %bitcast.73), channel_id=1, replica_groups=mesh['seq'=64,'exp'=2] {'seq'}, dimensions={0} | all-to-all | bytes 12582912 | tf_op jit(solution)/shard_map/all_to_all | solution.py:97
  175.4 26.4 %all-gather.2.cloned.1.call-done = bf16[3072,2048]{1,0:T(8,128)(2,1)} async-done(((bf16[1536,2048]{1,0:T(8,128)(2,1)}), bf16[3072,2048]{1,0:T(8,128)(2,1)}) %all-gather.2.cloned.1.call-update) | async-done | bytes 12582928 | tf_op jit(solution)/shard_map/all_gather | solution.py:101
  201.8 9.8 %fusion.14 = f32[3072,352]{0,1:T(8,128)} fusion(bf16[3072,2048]{1,0:T(8,128)(2,1)} %all-gather.2.cloned.1.call-done, bf16[1,2048,352]{1,2,0:T(8,128)(2,1)S(1)} %copy-done.8), kind=kOutput, calls=%fused_computation.23 | convolution fusion | flops 4429185024 | bytes 18350080 | tf_op jit(solution)/shard_map/dot_general | solution.py:102
  211.6 18.6 %convolution_convert_fusion = bf16[3072,2048]{1,0:T(8,128)(2,1)} fusion(bf16[3072,2048]{1,0:T(8,128)(2,1)} %all-gather.2.cloned.1.call-done, f32[3072,352]{0,1:T(8,128)} %fusion.14, bf16[1,352,2048]{2,1,0:T(8,128)(2,1)} %param.23, bf16[1,2048,352]{1,2,0:T(8,128)(2,1)} %param.22), kind=kOutput, calls=%fused_computation.4 | convolution fusion | flops 8871149568 | bytes 32374784 | tf_op jit(solution)/shard_map/dot_general | solution.py:106
  230.2 25.7 %reduce-scatter.2.cloned.1.call-done = bf16[1536,2048]{1,0:T(8,128)(2,1)} async-done(((bf16[3072,2048]{1,0:T(8,128)(2,1)}), bf16[1536,2048]{1,0:T(8,128)(2,1)}) %reduce-scatter.2.cloned.1.call-update) | async-done | bytes 6291472 | tf_op jit(solution)/shard_map/reduce_scatter | solution.py:105
  255.9 10.7 %all-to-all-start.1 = ((bf16[64,24,2048]{2,1,0:T(8,128)(2,1)}), bf16[64,24,2048]{2,1,0:T(8,128)(2,1)}, u32[]{:S(2)}, u32[]{:S(2)}) async-start(bf16[64,24,2048]{2,1,0:T(8,128)(2,1)} %bitcast.74), calls=%async_computation.2 | async-start | bytes 12582912 | tf_op jit(solution)/shard_map/all_to_all | solution.py:29
  266.8 88.4 %all-to-all-done.1 = bf16[64,24,2048]{2,1,0:T(8,128)(2,1)} async-done(((bf16[64,24,2048]{2,1,0:T(8,128)(2,1)}), bf16[64,24,2048]{2,1,0:T(8,128)(2,1)}, u32[]{:S(2)}, u32[]{:S(2)}) %all-to-all-start.1) | async-done | bytes 6291488 | tf_op jit(solution)/shard_map/all_to_all | solution.py:29
  355.2 10.8 %gather_fusion = bf16[768,2048]{1,0:T(8,128)(2,1)} fusion(bf16[1536,2048]{1,0:T(8,128)(2,1)} %bitcast.14, s32[1024]{0:T(1024)S(1)} %pad_clamp_fusion), kind=kCustom, calls=%fused_computation.1 | custom fusion | bytes 6294528 | tf_op jit(solution)/shard_map/gather | solution.py:113
  365.9 6.4 %reshape.179 = bf16[128,6,2048]{2,1,0:T(8,128)(2,1)} reshape(bf16[768,2048]{1,0:T(8,128)(2,1)} %gather_fusion) | data formatting | bytes 6291456 | tf_op jit(solution)/shard_map/reshape | solution.py:114
  372.4 3.5 fusion.33
  375.9 1.3 fusion.17
  (48 shorter events, 5.6 us)
Async XLA Ops:
  6.5 25.3 %copy-start = (bf16[512,2048]{1,0:T(8,128)(2,1)S(1)}, bf16[512,2048]{1,0:T(8,128)(2,1)}, u32[]{:S(2)}) copy-start(bf16[512,2048]{1,0:T(8,128)(2,1)} %param.17) | copy-start | bytes 6291460
  6.5 58.0 %all-reduce.3.cloned.1.call-start = ((), (), s32[]{:S(2)}) async-start(), calls=%async_computation.3 | async-start | bytes 2097152 | tf_op jit(solution)/shard_map/psum | solution.py:73
  8.9 15.7 %collective-permute-start = (bf16[2,256,512]{1,2,0:T(8,128)(2,1)S(1)}, bf16[2,256,512]{1,2,0:T(8,128)(2,1)}, u32[]{:S(2)}, u32[]{:S(2)}) collective-permute-start(bf16[2,256,512]{1,2,0:T(8,128)(2,1)S(1)} %pad_maximum_fusion.1), channel_id=1, source_target_pairs={{0,2},{2,4},{4,6},{6,8},{8,10},{10,12},{12,14},{14,16},{16,18},{18... | collective-permute-start | bytes 1572872 | tf_op jit(solution)/shard_map/ppermute | solution.py:19
  12.3 15.4 %collective-permute-start.1 = (bf16[2,256,512]{1,2,0:T(8,128)(2,1)S(1)}, bf16[2,256,512]{1,2,0:T(8,128)(2,1)}, u32[]{:S(2)}, u32[]{:S(2)}) collective-permute-start(bf16[2,256,512]{1,2,0:T(8,128)(2,1)S(1)} %pad_maximum_fusion.1), channel_id=1, source_target_pairs={{2,0},{4,2},{6,4},{8,6},{10,8},{12,10},{14,12},{16,14},{18,16},{20... | collective-permute-start | bytes 1572872 | tf_op jit(solution)/shard_map/ppermute | solution.py:21
  16.6 12.5 %copy-start.4 = (bf16[256,512]{1,0:T(8,128)(2,1)S(1)}, bf16[256,512]{1,0:T(8,128)(2,1)}, u32[]{:S(2)}) copy-start(bf16[256,512]{1,0:T(8,128)(2,1)} %param.12) | copy-start | bytes 786436
  31.8 1.9 copy-start.5
  31.8 32.8 %copy-start.2 = (bf16[128,2048]{1,0:T(8,128)(2,1)S(1)}, bf16[128,2048]{1,0:T(8,128)(2,1)}, u32[]{:S(2)}) copy-start(bf16[128,2048]{1,0:T(8,128)(2,1)} %param.15) | copy-start | bytes 1572868
  31.8 34.1 %copy-start.6 = (f32[2048]{0:T(1024)S(1)}, f32[2048]{0:T(1024)}, u32[]{:S(2)}) copy-start(f32[2048]{0:T(1024)} %param.18) | copy-start | bytes 24580
  33.6 168.2 %all-gather.2.cloned.1.call-start = ((), (), s32[]{:S(2)}) async-start(), calls=%async_computation.4 | async-start | bytes 18874368 | tf_op jit(solution)/shard_map/all_gather | solution.py:101
  175.3 26.5 %copy-start.8 = (bf16[1,2048,352]{1,2,0:T(8,128)(2,1)S(1)}, bf16[1,2048,352]{1,2,0:T(8,128)(2,1)}, u32[]{:S(2)}) copy-start(bf16[1,2048,352]{1,2,0:T(8,128)(2,1)} %param.21) | copy-start | bytes 4325380
  175.4 80.5 %reduce-scatter.2.cloned.1.call-start = ((), (), s32[]{:S(2)}) async-start(), calls=%async_computation.5 | async-start | bytes 18874368 | tf_op jit(solution)/shard_map/reduce_scatter | solution.py:105
  255.9 10.7 %copy-start.7 = (f32[128,6]{0,1:T(8,128)S(1)}, f32[128,6]{0,1:T(8,128)}, u32[]{:S(2)}) copy-start(f32[128,6]{0,1:T(8,128)} %param.20) | copy-start | bytes 9220
  255.9 99.3 %all-to-all-start.1 = ((bf16[64,24,2048]{2,1,0:T(8,128)(2,1)}), bf16[64,24,2048]{2,1,0:T(8,128)(2,1)}, u32[]{:S(2)}, u32[]{:S(2)}) async-start(bf16[64,24,2048]{2,1,0:T(8,128)(2,1)} %bitcast.74), calls=%async_computation.2 | async-start | bytes 12582912 | tf_op jit(solution)/shard_map/all_to_all | solution.py:29
  365.9 11.2 %copy-start.1 = (bf16[512,2048]{1,0:T(8,128)(2,1)S(1)}, bf16[512,2048]{1,0:T(8,128)(2,1)}, u32[]{:S(2)}) copy-start(bf16[512,2048]{1,0:T(8,128)(2,1)} %param.17) | copy-start | bytes 6291460
  372.4 3.5 copy-start.3
Sparse Core Ops, SparseCore 0:
  33.7 30.8 all-reduce.2
  175.5 26.2 all-gather.1
  230.3 25.5 reduce-scatter.1
where the time goes:
time: 384 us
  waiting for transfers between devices  180 us (47%)
  blocking collectives  84 us (22%)
  local copies, waits for them, and re-layouts  45.7 us (12%)
  matrix products  34.6 us (9%)
  starting transfers between devices  16.6 us (4%)
  between operations  13.4 us (3%)
  other arithmetic  9.89 us (3%)
    all_to_all x1, waiting for transfers between devices, send_back(): lax.all_to_all(result, 'seq', split_axis=0, concat_axis=0, tiled=True)  88.4 us
    all_to_all x1, blocking collectives, shards(): lax.all_to_all(outgoing, 'seq', split_axis=0, concat_axis=0, tiled=True)  84 us
    psum x1, waiting for transfers between devices, shards(): lax.psum(jnp.dot(attended, out_weight, preferred_element_type=jnp.float32...  28 us
    all_gather x1, waiting for transfers between devices, shards(): group = lax.all_gather(inputs, 'exp', axis=0, tiled=True)  26.4 us
    reduce_scatter x1, waiting for transfers between devices, shards(): lax.psum_scatter(jnp.dot(act, w_down[0], preferred_element_type=jnp.float...  25.7 us
    scatter x1, local copies, waits for them, and re-layouts, shards(): outgoing = jnp.zeros((n_experts * capacity, normed.shape[1]), jnp.bfloat1...  24.2 us
    dot_general x1, matrix products, shards(): jnp.dot(act, w_down[0], preferred_element_type=jnp.float32)  18.6 us
    gather x1, local copies, waits for them, and re-layouts, shards(): gathered = back.reshape(n_experts * capacity, back.shape[2])[destination]  10.8 us
  transfers between devices with their start and end apart: 6, of which 6 were waited for; matrix products, arithmetic and copies ran while one was open for 1% of the time, Pallas kernels for 0%

commit v1 on v0

--- a/solution.py
+++ b/solution.py
@@ -98,7 +98,9 @@
     sources = arrived.shape[0]
     slots = arrived.shape[1]
     inputs = arrived.reshape(sources * slots, arrived.shape[2])
-    group = lax.all_gather(inputs, "exp", axis=0, tiled=True)
+    world = lax.axis_size("exp")
+    rack = [world if w == 0 else 1 for w in range(inputs.ndim)]
+    group = lax.all_to_all(jnp.tile(inputs, rack), "exp", split_axis=0, concat_axis=0, tiled=True)
     gate_part = jnp.dot(group, w_gate[0], preferred_element_type=jnp.float32)
     up_part = jnp.dot(group, w_up[0], preferred_element_type=jnp.float32)
     act = (jax.nn.silu(gate_part) * up_part).astype(jnp.bfloat16)

time: 384 us -> 372 us (0.969)
  waiting for transfers between devices: 180 us -> 151 us
  blocking collectives: 84 us -> 97.8 us
  local copies, waits for them, and re-layouts: 45.7 us -> 51.7 us
    all_gather x1 -> x0, waiting for transfers between devices: 26.4 us -> none  [shards(): group = lax.all_gather(inputs, 'exp', axis=0, tiled=True)]
    all_to_all x0 -> x1, blocking collectives: none -> 14 us  [shards(): lax.all_to_all(jnp.tile(inputs, rack), 'exp', split_axis=0, concat_axis=0...]
    unnamed x22 -> x24, local copies, waits for them, and re-layouts: 2.62 us -> 7.1 us
  transfers between devices with their start and end apart: 6 -> 5, of which waited for: 6 -> 5; matrix products, arithmetic and copies ran while one was open for 1% -> 1% of each run, Pallas kernels for 0% -> 0%
where the time goes in v1:
time: 372 us
  waiting for transfers between devices  151 us (41%)
  blocking collectives  97.8 us (26%)
  local copies, waits for them, and re-layouts  51.7 us (14%)
  matrix products  31.2 us (8%)
  starting transfers between devices  16.6 us (4%)
  between operations  13.7 us (4%)
  other arithmetic  9.89 us (3%)
    all_to_all x1, waiting for transfers between devices, send_back(): lax.all_to_all(result, 'seq', split_axis=0, concat_axis=0, tiled=True)  88.8 us
    all_to_all x1, blocking collectives, shards(): lax.all_to_all(outgoing, 'seq', split_axis=0, concat_axis=0, tiled=True)  83.9 us
    psum x1, waiting for transfers between devices, shards(): lax.psum(jnp.dot(attended, out_weight, preferred_element_type=jnp.float32...  28 us
    scatter x1, local copies, waits for them, and re-layouts, shards(): outgoing = jnp.zeros((n_experts * capacity, normed.shape[1]), jnp.bfloat1...  24.2 us
    reduce_scatter x1, waiting for transfers between devices, shards(): lax.psum_scatter(jnp.dot(act, w_down[0], preferred_element_type=jnp.float...  23 us
    dot_general x1, matrix products, shards(): jnp.dot(act, w_down[0], preferred_element_type=jnp.float32)  18.7 us
    all_to_all x1, blocking collectives, shards(): lax.all_to_all(jnp.tile(inputs, rack), 'exp', split_axis=0, concat_axis=0...  14 us
    gather x1, local copies, waits for them, and re-layouts, shards(): gathered = back.reshape(n_experts * capacity, back.shape[2])[destination]  10.8 us
  transfers between devices with their start and end apart: 5, of which 5 were waited for; matrix products, arithmetic and copies ran while one was open for 1% of the time, Pallas kernels for 0%

profile of v1, /device:TPU:10, one launch (start us, length us, event | category | flops | bytes accessed | tf_op | source)
XLA Modules:
  0.0 371.7 jit_solution(6378567580375284651)
XLA Ops:
  8.9 3.4 collective-permute-start
  12.3 2.4 collective-permute-start.1
  16.6 7.9 %collective-permute-done = bf16[2,256,512]{1,2,0:T(8,128)(2,1)} collective-permute-done((bf16[2,256,512]{1,2,0:T(8,128)(2,1)S(1)}, bf16[2,256,512]{1,2,0:T(8,128)(2,1)}, u32[]{:S(2)}, u32[]{:S(2)}) %collective-permute-start) | collective-permute-done | bytes 524320 | tf_op jit(solution)/shard_map/ppermute | solution.py:19
  24.6 3.1 collective-permute-done.1
  27.7 1.3 pad_maximum_fusion
  29.8 1.6 fusion.32
  31.8 1.7 convolution_convert_fusion.1
  34.1 1.8 reduce-window.6
  36.6 28.0 %all-reduce.3.cloned.1.call-done = bf16[256,2048]{1,0:T(8,128)(2,1)} async-done(((bf16[256,2048]{1,0:T(8,128)(2,1)}), bf16[256,2048]{1,0:T(8,128)(2,1)}) %all-reduce.3.cloned.1.call-update) | async-done | bytes 1048592 | tf_op jit(solution)/shard_map/psum | solution.py:73
  64.6 1.3 multiply_reduce_fusion
  67.2 24.2 %scatter_custom_fusion = bf16[1536,2048]{1,0:T(8,128)(2,1)} fusion(s32[768]{0:T(1024)S(1)} %fusion.26, bf16[128,2048]{1,0:T(8,128)(2,1)S(1)} %multiply_convert_fusion, s32[1024]{0:T(1024)S(1)} %pad_clamp_fusion.1, bf16[]{:T(256)} %constant.50.clone.1), kind=kCustom, calls=%fused_computation.8 | custom fusion | bytes 6291458 | tf_op jit(solution)/shard_map/scatter | solution.py:94
  91.4 83.9 %all_to_all.19 = bf16[64,24,2048]{2,1,0:T(8,128)(2,1)S(1)} all-to-all(bf16[64,24,2048]{2,1,0:T(8,128)(2,1)} %bitcast.73), channel_id=1, replica_groups=mesh['seq'=64,'exp'=2] {'seq'}, dimensions={0} | all-to-all | bytes 12582912 | tf_op jit(solution)/shard_map/all_to_all | solution.py:97
  175.2 1.5 tile.9
  176.8 14.0 %all_to_all.20 = bf16[2,1536,2048]{2,1,0:T(8,128)(2,1)S(1)} all-to-all(bf16[2,1536,2048]{2,1,0:T(8,128)(2,1)S(1)} %tile.9), channel_id=1, replica_groups=mesh['seq'=64,'exp'=2] {'exp'}, dimensions={0} | all-to-all | bytes 25165824 | tf_op jit(solution)/shard_map/all_to_all | solution.py:103
  190.8 4.5 %copy-done.2 = bf16[2,1536,2048]{2,1,0:T(8,128)(2,1)} copy-done((bf16[2,1536,2048]{2,1,0:T(8,128)(2,1)}, bf16[2,1536,2048]{2,1,0:T(8,128)(2,1)S(1)}, u32[]{:S(2)}) %copy-start.2) | copy-done | bytes 12582936
  195.3 6.3 %fusion.14 = f32[3072,352]{0,1:T(8,128)} fusion(bf16[3072,2048]{1,0:T(8,128)(2,1)S(1)} %bitcast.75, bf16[1,2048,352]{1,2,0:T(8,128)(2,1)S(1)} %copy-done.9), kind=kOutput, calls=%fused_computation.23 | convolution fusion | flops 4429185024 | bytes 18350080 | tf_op jit(solution)/shard_map/dot_general | solution.py:104
  201.6 18.7 %convolution_convert_fusion = bf16[3072,2048]{1,0:T(8,128)(2,1)} fusion(bf16[3072,2048]{1,0:T(8,128)(2,1)} %bitcast.76, f32[3072,352]{0,1:T(8,128)} %fusion.14, bf16[1,352,2048]{2,1,0:T(8,128)(2,1)} %param.23, bf16[1,2048,352]{1,2,0:T(8,128)(2,1)} %param.22), kind=kOutput, calls=%fused_computation.4 | convolution fusion | flops 8871149568 | bytes 32374784 | tf_op jit(solution)/shard_map/dot_general | solution.py:108
  220.2 23.0 %reduce-scatter.2.cloned.1.call-done = bf16[1536,2048]{1,0:T(8,128)(2,1)} async-done(((bf16[3072,2048]{1,0:T(8,128)(2,1)}), bf16[1536,2048]{1,0:T(8,128)(2,1)}) %reduce-scatter.2.cloned.1.call-update) | async-done | bytes 6291472 | tf_op jit(solution)/shard_map/reduce_scatter | solution.py:107
  243.2 10.7 %all-to-all-start.2 = ((bf16[64,24,2048]{2,1,0:T(8,128)(2,1)}), bf16[64,24,2048]{2,1,0:T(8,128)(2,1)}, u32[]{:S(2)}, u32[]{:S(2)}) async-start(bf16[64,24,2048]{2,1,0:T(8,128)(2,1)} %bitcast.77), calls=%async_computation.3 | async-start | bytes 12582912 | tf_op jit(solution)/shard_map/all_to_all | solution.py:29
  254.1 88.8 %all-to-all-done.2 = bf16[64,24,2048]{2,1,0:T(8,128)(2,1)} async-done(((bf16[64,24,2048]{2,1,0:T(8,128)(2,1)}), bf16[64,24,2048]{2,1,0:T(8,128)(2,1)}, u32[]{:S(2)}, u32[]{:S(2)}) %all-to-all-start.2) | async-done | bytes 6291488 | tf_op jit(solution)/shard_map/all_to_all | solution.py:29
  342.9 10.8 %gather_fusion = bf16[768,2048]{1,0:T(8,128)(2,1)} fusion(bf16[1536,2048]{1,0:T(8,128)(2,1)} %bitcast.15, s32[1024]{0:T(1024)S(1)} %pad_clamp_fusion), kind=kCustom, calls=%fused_computation.1 | custom fusion | bytes 6294528 | tf_op jit(solution)/shard_map/gather | solution.py:115
  353.7 6.4 %reshape.182 = bf16[128,6,2048]{2,1,0:T(8,128)(2,1)} reshape(bf16[768,2048]{1,0:T(8,128)(2,1)} %gather_fusion) | data formatting | bytes 6291456 | tf_op jit(solution)/shard_map/reshape | solution.py:116
  360.1 3.5 fusion.33
  363.6 1.3 fusion.17
  (49 shorter events, 8.0 us)
Async XLA Ops:
  6.5 25.3 %copy-start = (bf16[512,2048]{1,0:T(8,128)(2,1)S(1)}, bf16[512,2048]{1,0:T(8,128)(2,1)}, u32[]{:S(2)}) copy-start(bf16[512,2048]{1,0:T(8,128)(2,1)} %param.17) | copy-start | bytes 6291460
  6.5 58.0 %all-reduce.3.cloned.1.call-start = ((), (), s32[]{:S(2)}) async-start(), calls=%async_computation.4 | async-start | bytes 2097152 | tf_op jit(solution)/shard_map/psum | solution.py:73
  8.9 15.7 %collective-permute-start = (bf16[2,256,512]{1,2,0:T(8,128)(2,1)S(1)}, bf16[2,256,512]{1,2,0:T(8,128)(2,1)}, u32[]{:S(2)}, u32[]{:S(2)}) collective-permute-start(bf16[2,256,512]{1,2,0:T(8,128)(2,1)S(1)} %pad_maximum_fusion.1), channel_id=1, source_target_pairs={{0,2},{2,4},{4,6},{6,8},{8,10},{10,12},{12,14},{14,16},{16,18},{18... | collective-permute-start | bytes 1572872 | tf_op jit(solution)/shard_map/ppermute | solution.py:19
  12.3 15.4 %collective-permute-start.1 = (bf16[2,256,512]{1,2,0:T(8,128)(2,1)S(1)}, bf16[2,256,512]{1,2,0:T(8,128)(2,1)}, u32[]{:S(2)}, u32[]{:S(2)}) collective-permute-start(bf16[2,256,512]{1,2,0:T(8,128)(2,1)S(1)} %pad_maximum_fusion.1), channel_id=1, source_target_pairs={{2,0},{4,2},{6,4},{8,6},{10,8},{12,10},{14,12},{16,14},{18,16},{20... | collective-permute-start | bytes 1572872 | tf_op jit(solution)/shard_map/ppermute | solution.py:21
  16.6 12.5 %copy-start.5 = (bf16[256,512]{1,0:T(8,128)(2,1)S(1)}, bf16[256,512]{1,0:T(8,128)(2,1)}, u32[]{:S(2)}) copy-start(bf16[256,512]{1,0:T(8,128)(2,1)} %param.12) | copy-start | bytes 786436
  31.8 1.9 copy-start.6
  31.8 32.8 %copy-start.3 = (bf16[128,2048]{1,0:T(8,128)(2,1)S(1)}, bf16[128,2048]{1,0:T(8,128)(2,1)}, u32[]{:S(2)}) copy-start(bf16[128,2048]{1,0:T(8,128)(2,1)} %param.15) | copy-start | bytes 1572868
  31.8 34.1 %copy-start.7 = (f32[2048]{0:T(1024)S(1)}, f32[2048]{0:T(1024)}, u32[]{:S(2)}) copy-start(f32[2048]{0:T(1024)} %param.18) | copy-start | bytes 24580
  33.6 209.7 %reduce-scatter.2.cloned.1.call-start = ((), (), s32[]{:S(2)}) async-start(), calls=%async_computation.5 | async-start | bytes 18874368 | tf_op jit(solution)/shard_map/reduce_scatter | solution.py:107
  176.8 18.5 %copy-start.9 = (bf16[1,2048,352]{1,2,0:T(8,128)(2,1)S(1)}, bf16[1,2048,352]{1,2,0:T(8,128)(2,1)}, u32[]{:S(2)}) copy-start(bf16[1,2048,352]{1,2,0:T(8,128)(2,1)} %param.21) | copy-start | bytes 4325380
  190.8 4.5 %copy-start.2 = (bf16[2,1536,2048]{2,1,0:T(8,128)(2,1)}, bf16[2,1536,2048]{2,1,0:T(8,128)(2,1)S(1)}, u32[]{:S(2)}) copy-start(bf16[2,1536,2048]{2,1,0:T(8,128)(2,1)S(1)} %all_to_all.20) | copy-start | bytes 37748740
  243.2 10.7 %copy-start.8 = (f32[128,6]{0,1:T(8,128)S(1)}, f32[128,6]{0,1:T(8,128)}, u32[]{:S(2)}) copy-start(f32[128,6]{0,1:T(8,128)} %param.20) | copy-start | bytes 9220
  243.2 99.6 %all-to-all-start.2 = ((bf16[64,24,2048]{2,1,0:T(8,128)(2,1)}), bf16[64,24,2048]{2,1,0:T(8,128)(2,1)}, u32[]{:S(2)}, u32[]{:S(2)}) async-start(bf16[64,24,2048]{2,1,0:T(8,128)(2,1)} %bitcast.77), calls=%async_computation.3 | async-start | bytes 12582912 | tf_op jit(solution)/shard_map/all_to_all | solution.py:29
  353.7 11.2 %copy-start.1 = (bf16[512,2048]{1,0:T(8,128)(2,1)S(1)}, bf16[512,2048]{1,0:T(8,128)(2,1)}, u32[]{:S(2)}) copy-start(bf16[512,2048]{1,0:T(8,128)(2,1)} %param.17) | copy-start | bytes 6291460
  360.1 3.5 copy-start.4
Sparse Core Ops, SparseCore 0:
  33.7 30.8 all-reduce.2
  220.3 22.8 reduce-scatter.1
